TPU v7x, 512 devices: a whole 4x8x8 slice. The times are simulated.
512 devices in a mesh: dp: 64 (over z, y_hi, x), shard: 8 (over y_lo, core).
Axes of the slice: x: 4, y: 8 (y_hi: 2, y_lo: 4; y = y_hi * 4 + y_lo), z: 8, core: 2. Of those that a mesh axis runs over, the one named last changes fastest.
Arguments:
- inputs: bfloat16 [512, 8, 8, 8, 256], P(('dp', 'shard')), may hold values from -24 to 24
- cotangent: bfloat16 [512, 4, 4, 4, 256], P(('dp', 'shard')), may hold values from -6 to 6
- weights: bfloat16 [28, 256, 256], P(None, 'shard'), may hold values from -0.078125 to 0.078125
Outputs:
- outputs: bfloat16 [512, 4, 4, 4, 256], P(('dp', 'shard'))
- input_grad: bfloat16 [512, 8, 8, 8, 256], P(('dp', 'shard'))
- weight_grad: float32 [28, 256, 256], P(None, 'shard')
All inputs are finite; a program needn't handle non-finite values.
Results may differ from a plain program's by a relative error of at most 0.012.
Values may be sent and summed in bfloat16 or wider, within the bound.
A program may use at most 64 MiB of HBM per device.

v0:
```python
import jax
import jax.numpy as jnp
from jax import lax
from jax.sharding import PartitionSpec as P


def build_cols(values):
    edge = values.shape[0]
    half = edge // 2
    width = values.shape[3]
    act = jax.nn.silu(values.astype(jnp.float32)).astype(jnp.bfloat16)
    padded = jnp.pad(act, ((1, 1), (1, 1), (1, 1), (0, 0)))
    pieces = []
    for first in range(3):
        for second in range(3):
            for third in range(3):
                pieces.append(
                    padded[
                        first : first + edge : 2,
                        second : second + edge : 2,
                        third : third + edge : 2,
                    ]
                )
    pieces.append(values[0::2, 0::2, 0::2])
    return jnp.stack(pieces, axis=3).reshape(half * half * half, 28, width)


def spread_back(values, grad_rows, piece, half):
    width = piece.shape[1]
    edge = 2 * half
    grid = jnp.zeros((edge + 2, edge + 2, edge + 2, width), jnp.float32)
    for first in range(3):
        block = jnp.einsum(
            "qo,tco->qtc",
            grad_rows,
            piece[9 * first : 9 * first + 9],
            preferred_element_type=jnp.float32,
        )
        block = block.reshape(half, half, half, 9, width)
        for second in range(3):
            for third in range(3):
                grid = grid.at[
                    first : first + edge : 2, second : second + edge : 2, third : third + edge : 2
                ].add(block[:, :, :, 3 * second + third])
    direct = jnp.einsum(
        "qo,co->qc", grad_rows, piece[27], preferred_element_type=jnp.float32
    ).reshape(half, half, half, width)
    own = values.astype(jnp.float32)
    sigma = jax.nn.sigmoid(own)
    grad_in = grid[1:-1, 1:-1, 1:-1] * sigma * (1.0 + own * (1.0 - sigma))
    grad_in = grad_in.at[0::2, 0::2, 0::2].add(direct)
    return grad_in.astype(jnp.bfloat16)


def shards(inputs, cotangent, weights):
    values = inputs[0]
    edge = values.shape[0]
    half = edge // 2
    chans = values.shape[3]
    taps_count = weights.shape[0]
    cols = build_cols(values)
    grad_rows = cotangent[0].reshape(half * half * half, chans)
    result = jnp.einsum(
        "qtc,tco->qo",
        cols,
        lax.all_gather(weights, "shard", axis=1, tiled=True),
        preferred_element_type=jnp.float32,
    )
    grad_in = spread_back(
        values, grad_rows, lax.all_gather(weights, "shard", axis=1, tiled=True), half
    )
    term = lax.dot_general(
        cols.reshape(half * half * half, taps_count * chans),
        grad_rows,
        (((0,), (0,)), ((), ())),
        preferred_element_type=jnp.float32,
    )
    term = term.astype(jnp.bfloat16).astype(jnp.float32).reshape(taps_count, chans, chans)
    owned = lax.psum_scatter(
        term.astype(jnp.bfloat16), "shard", scatter_dimension=1, tiled=True
    ).astype(jnp.float32)
    weight_grad = lax.psum(owned, "dp")
    outputs = result.astype(jnp.bfloat16).reshape(1, half, half, half, chans)
    return (outputs, grad_in.reshape(1, edge, edge, edge, chans), weight_grad)


def solution(mesh):
    return jax.shard_map(
        shards,
        mesh=mesh,
        in_specs=(
            P(("dp", "shard"), None, None, None, None),
            P(("dp", "shard"), None, None, None, None),
            P(None, "shard", None),
        ),
        out_specs=(
            P(("dp", "shard"), None, None, None, None),
            P(("dp", "shard"), None, None, None, None),
            P(None, "shard", None),
        ),
        check_vma=False,
    )
```

profile of v0, /device:TPU:8, one launch (start us, length us, event | category | flops | bytes accessed | tf_op | source)
XLA Modules:
  0.0 727.1 jit_solution(8520491467379494696)
XLA Ops:
  7.2 0.7 all-gather.2.cloned.1.call-update
  10.8 5.8 slice.207
  16.6 0.8 reshape_squeeze.3
  17.4 45.1 %all-gather.2.cloned.1.call-done = bf16[28,256,256]{2,1,0:T(8,128)(2,1)} async-done(((bf16[28,32,256]{2,1,0:T(8,128)(2,1)}), bf16[28,256,256]{2,1,0:T(8,128)(2,1)}) %all-gather.2.cloned.1.call-update) | async-done | bytes 3670032 | tf_op jit(solution)/shard_map/all_gather | solution.py:66
  62.5 1.8 fusion.2
  64.5 0.7 reshape.87
  65.4 1.8 fusion.1
  67.6 1.8 fusion
  70.1 5.2 scatter_fusion
  75.3 4.8 scatter_fusion.1
  80.1 4.8 scatter_fusion.2
  84.9 4.8 scatter_fusion.3
  89.7 4.8 scatter_fusion.4
  94.6 4.8 scatter_fusion.5
  99.3 4.8 scatter_fusion.6
  104.2 4.8 scatter_fusion.7
  109.0 4.8 scatter_fusion.8
  113.8 5.3 scatter_fusion.9
  119.0 4.8 scatter_fusion.10
  123.9 4.8 scatter_fusion.11
  128.6 4.8 scatter_fusion.12
  133.5 4.8 scatter_fusion.13
  138.3 4.8 scatter_fusion.14
  143.0 4.8 scatter_fusion.15
  147.9 4.8 scatter_fusion.16
  152.7 4.8 scatter_fusion.17
  157.5 4.8 scatter_fusion.18
  162.3 4.8 scatter_fusion.19
  167.1 4.9 scatter_fusion.20
  172.1 4.8 scatter_fusion.21
  176.9 4.8 scatter_fusion.22
  181.7 4.8 scatter_fusion.23
  186.5 4.8 scatter_fusion.24
  191.3 4.8 scatter_fusion.25
  196.1 4.8 scatter_fusion.26
  202.1 0.4 slice.182
  203.4 0.4 slice.185
  204.6 0.4 slice.188
  205.1 0.4 slice.189
  205.5 0.4 slice.190
  205.9 0.4 slice.191
  206.3 0.4 slice.192
  206.8 0.4 slice.193
  207.2 0.4 slice.194
  207.6 0.4 slice.195
  208.0 0.4 slice.196
  208.4 0.4 slice.197
  208.9 0.4 slice.198
  209.3 0.4 slice.199
  209.7 0.4 slice.200
  211.0 0.4 slice.203
  211.4 0.4 slice.204
  211.8 0.4 slice.205
  212.3 0.6 slice.206
  213.7 0.5 copy.6
  214.2 0.5 copy.12
  214.7 3.0 convolution_convert_fusion
  218.9 2.8 fusion.3
  221.7 0.6 reshape.83
  222.3 1.1 fusion.10
  223.5 4.6 scatter_fusion.27
  228.1 0.7 convert_bitcast_fusion
  228.8 41.0 %reduce-scatter.2.cloned.1.call-done = bf16[28,32,256]{2,1,0:T(8,128)(2,1)} async-done(((bf16[28,256,256]{2,1,0:T(8,128)(2,1)}), bf16[28,32,256]{2,1,0:T(8,128)(2,1)}) %reduce-scatter.2.cloned.1.call-update) | async-done | bytes 458768 | tf_op jit(solution)/shard_map/reduce_scatter | solution.py:79
  269.8 450.2 %all-reduce.2 = f32[28,32,256]{2,1,0:T(8,128)} all-reduce(bf16[28,32,256]{2,1,0:T(8,128)(2,1)} %reduce-scatter.2.cloned.1.call-done), channel_id=1, replica_groups=mesh['dp'=64,'shard'=8] {'dp'}, use_global_device_ids=true, to_apply=%region_29.30 | all-reduce | flops 229376 | bytes 1376256 | tf_op jit(solution)/shard_map/psum | solution.py:82
  (172 shorter events, 9.2 us)
Async XLA Ops:
  7.2 55.4 %all-gather.2.cloned.1.call-start = ((), (), s32[]{:S(2)}) async-start(), calls=%async_computation.1 | async-start | bytes 4128768 | tf_op jit(solution)/shard_map/all_gather | solution.py:66
  7.9 261.9 %reduce-scatter.2.cloned.1.call-start = ((), (), s32[]{:S(2)}) async-start(), calls=%async_computation.2 | async-start | bytes 4128768 | tf_op jit(solution)/shard_map/reduce_scatter | solution.py:79
  64.3 1.1 copy-start
  186.5 14.4 %copy-start.1 = (bf16[1,8,8,8,256]{4,3,2,1,0:T(8,128)(2,1)S(1)}, bf16[1,8,8,8,256]{4,3,2,1,0:T(8,128)(2,1)}, u32[]{:S(2)}) copy-start(bf16[1,8,8,8,256]{4,3,2,1,0:T(8,128)(2,1)} %param.3) | copy-start | bytes 786436
Sparse Core Ops, SparseCore 0:
  10.1 52.4 all-gather.1
  217.9 51.8 reduce-scatter.1
where the time goes:
time: 737 us; the launch traced here: 727 us
  blocking collectives  450 us (61%)
  other arithmetic  137 us (19%)
  waiting for transfers between devices  86.8 us (12%)
  local copies, waits for them, and re-layouts  25.5 us (3%)
  between operations  15.7 us (2%)
  matrix products  12.2 us (2%)
    psum x1, blocking collectives, shards(): weight_grad = lax.psum(owned, 'dp')  450 us
    scatter-add x27, other arithmetic, spread_back(): grid = grid.at[first:first + edge:2, second:second + edge:2, third:third...  131 us
    all_gather x1, waiting for transfers between devices, shards(): lax.all_gather(weights, 'shard', axis=1, tiled=True)  45.1 us
    reduce_scatter x1, waiting for transfers between devices, shards(): lax.psum_scatter(term.astype(jnp.bfloat16), 'shard', scatter_dimension=1,...  41 us
  transfers between devices with their start and end apart: 2, of which 2 were waited for; matrix products, arithmetic and copies ran while one was open for 3% of the time, Pallas kernels for 0%

commit v1 on v0

--- a/solution.py
+++ b/solution.py
@@ -2,6 +2,11 @@
 import jax.numpy as jnp
 from jax import lax
 from jax.sharding import PartitionSpec as P
+
+
+def gather_over(shard, axis, dim):
+    sent = jnp.stack([shard] * lax.axis_size(axis))
+    return jnp.concatenate(lax.all_to_all(sent, axis, 0, 0), axis=dim)
 
 
 def build_cols(values):
@@ -61,10 +66,7 @@
     cols = build_cols(values)
     grad_rows = cotangent[0].reshape(half * half * half, chans)
     result = jnp.einsum(
-        "qtc,tco->qo",
-        cols,
-        lax.all_gather(weights, "shard", axis=1, tiled=True),
-        preferred_element_type=jnp.float32,
+        "qtc,tco->qo", cols, gather_over(weights, "shard", 1), preferred_element_type=jnp.float32
     )
     grad_in = spread_back(
         values, grad_rows, lax.all_gather(weights, "shard", axis=1, tiled=True), half

time: 737 us -> 811 us (1.10)
  waiting for transfers between devices: 86.8 us -> 148 us
  starting transfers between devices: 0.08 us -> 10.3 us
    all_gather x1, waiting for transfers between devices: 45.1 us -> 104 us  [shards(): lax.all_gather(weights, 'shard', axis=1, tiled=True)]
    all_to_all x0 -> x1, starting transfers between devices: none -> 10.3 us  [gather_over(): return jnp.concatenate(lax.all_to_all(sent, axis, 0, 0), axis=dim)]
  transfers between devices with their start and end apart: 2 -> 3, of which waited for: 2 -> 2; matrix products, arithmetic and copies ran while one was open for 3% -> 22% of each run, Pallas kernels for 0% -> 0%
where the time goes in v1:
time: 811 us; the launch traced here: 801 us
  blocking collectives  450 us (55%)
  waiting for transfers between devices  148 us (18%)
  other arithmetic  138 us (17%)
  local copies, waits for them, and re-layouts  28.3 us (3%)
  between operations  15.7 us (2%)
  starting transfers between devices  10.3 us (1%)
  matrix products  10.2 us (1%)
    psum x1, blocking collectives, shards(): weight_grad = lax.psum(owned, 'dp')  450 us
    scatter-add x27, other arithmetic, spread_back(): grid = grid.at[first:first + edge:2, second:second + edge:2, third:third...  132 us
    all_gather x1, waiting for transfers between devices, shards(): lax.all_gather(weights, 'shard', axis=1, tiled=True)  104 us
    reduce_scatter x1, waiting for transfers between devices, shards(): lax.psum_scatter(term.astype(jnp.bfloat16), 'shard', scatter_dimension=1,...  42.8 us
  transfers between devices with their start and end apart: 3, of which 2 were waited for; matrix products, arithmetic and copies ran while one was open for 22% of the time, Pallas kernels for 0%

profile of v1, /device:TPU:8, one launch (start us, length us, event | category | flops | bytes accessed | tf_op | source)
XLA Modules:
  0.0 800.7 jit_solution(5872317585293864474)
XLA Ops:
  7.2 0.7 all-gather.2.cloned.1.call-update
  7.9 3.4 stack.185
  11.3 10.3 %all-to-all-start = ((bf16[8,28,32,256]{3,2,1,0:T(8,128)(2,1)}), bf16[8,28,32,256]{3,2,1,0:T(8,128)(2,1)}, u32[]{:S(2)}, u32[]{:S(2)}) async-start(bf16[8,28,32,256]{3,2,1,0:T(8,128)(2,1)} %stack.185), calls=%async_computation | async-start | bytes 7340032 | tf_op jit(solution)/shard_map/all_to_all | solution.py:9
  21.6 0.4 slice.207
  22.1 0.6 reshape_squeeze.3
  25.6 104.4 %all-gather.2.cloned.1.call-done = bf16[28,256,256]{2,1,0:T(8,128)(2,1)} async-done(((bf16[28,32,256]{2,1,0:T(8,128)(2,1)}), bf16[28,256,256]{2,1,0:T(8,128)(2,1)}) %all-gather.2.cloned.1.call-update) | async-done | bytes 3670032 | tf_op jit(solution)/shard_map/all_gather | solution.py:72
  129.9 1.8 fusion
  132.1 1.8 fusion.2
  134.1 1.8 fusion.1
  136.4 0.6 reshape.121
  137.0 0.7 reshape.115
  137.7 0.6 reshape.109
  138.3 0.7 reshape.103
  139.0 0.7 reshape.97
  139.8 5.2 scatter_fusion
  145.1 5.2 scatter_fusion.1
  150.3 5.2 scatter_fusion.2
  155.5 5.2 scatter_fusion.3
  160.8 5.2 scatter_fusion.4
  166.0 4.8 scatter_fusion.5
  170.8 4.8 scatter_fusion.6
  175.6 4.8 scatter_fusion.7
  180.4 5.2 scatter_fusion.8
  185.7 4.8 scatter_fusion.9
  190.5 4.8 scatter_fusion.10
  195.3 4.8 scatter_fusion.11
  200.1 4.8 scatter_fusion.12
  204.9 4.8 scatter_fusion.13
  209.7 4.8 scatter_fusion.14
  214.5 4.8 scatter_fusion.15
  219.3 4.8 scatter_fusion.16
  224.1 4.8 scatter_fusion.17
  228.9 4.8 scatter_fusion.18
  233.7 5.0 scatter_fusion.19
  238.7 4.8 scatter_fusion.20
  243.5 4.8 scatter_fusion.21
  248.3 4.8 scatter_fusion.22
  253.1 4.8 scatter_fusion.23
  257.9 4.8 scatter_fusion.24
  262.7 4.8 scatter_fusion.25
  267.5 4.8 scatter_fusion.26
  273.6 0.4 slice.194
  274.0 0.4 slice.193
  274.4 0.4 slice.192
  274.8 0.4 slice.191
  275.7 0.4 slice.189
  276.1 0.4 slice.188
  277.4 0.4 slice.185
  278.6 0.4 slice.182
  280.3 0.4 slice.206
  281.6 0.4 slice.203
  282.8 0.4 slice.200
  284.1 0.6 slice.197
  285.1 0.5 copy.8
  285.6 0.5 copy.14
  286.2 3.1 convolution_convert_fusion
  290.1 1.1 fusion.10
  291.2 2.4 copy.7
  294.0 0.8 fusion.3
  294.8 0.6 reshape.93
  295.4 4.6 scatter_fusion.27
  300.0 0.7 convert_bitcast_fusion
  300.8 42.8 %reduce-scatter.2.cloned.1.call-done = bf16[28,32,256]{2,1,0:T(8,128)(2,1)} async-done(((bf16[28,256,256]{2,1,0:T(8,128)(2,1)}), bf16[28,32,256]{2,1,0:T(8,128)(2,1)}) %reduce-scatter.2.cloned.1.call-update) | async-done | bytes 458768 | tf_op jit(solution)/shard_map/reduce_scatter | solution.py:81
  343.6 450.1 %all-reduce.2 = f32[28,32,256]{2,1,0:T(8,128)} all-reduce(bf16[28,32,256]{2,1,0:T(8,128)(2,1)} %reduce-scatter.2.cloned.1.call-done), channel_id=1, replica_groups=mesh['dp'=64,'shard'=8] {'dp'}, use_global_device_ids=true, to_apply=%region_29.30 | all-reduce | flops 229376 | bytes 1376256 | tf_op jit(solution)/shard_map/psum | solution.py:84
  (178 shorter events, 11.8 us)
Async XLA Ops:
  7.2 122.8 %all-gather.2.cloned.1.call-start = ((), (), s32[]{:S(2)}) async-start(), calls=%async_computation.2 | async-start | bytes 4128768 | tf_op jit(solution)/shard_map/all_gather | solution.py:72
  11.3 10.3 %copy-start.1 = (bf16[1,8,8,8,256]{4,3,2,1,0:T(8,128)(2,1)S(1)}, bf16[1,8,8,8,256]{4,3,2,1,0:T(8,128)(2,1)}, u32[]{:S(2)}) copy-start(bf16[1,8,8,8,256]{4,3,2,1,0:T(8,128)(2,1)} %param.3) | copy-start | bytes 786436
  11.3 10.8 %copy-start = (bf16[1,4,4,4,256]{4,3,2,1,0:T(4,128)(2,1)S(1)}, bf16[1,4,4,4,256]{4,3,2,1,0:T(4,128)(2,1)}, u32[]{:S(2)}) copy-start(bf16[1,4,4,4,256]{4,3,2,1,0:T(4,128)(2,1)} %param.4) | copy-start | bytes 98308
  11.3 279.9 %all-to-all-start = ((bf16[8,28,32,256]{3,2,1,0:T(8,128)(2,1)}), bf16[8,28,32,256]{3,2,1,0:T(8,128)(2,1)}, u32[]{:S(2)}, u32[]{:S(2)}) async-start(bf16[8,28,32,256]{3,2,1,0:T(8,128)(2,1)} %stack.185), calls=%async_computation | async-start | bytes 7340032 | tf_op jit(solution)/shard_map/all_to_all | solution.py:9
  21.6 322.0 %reduce-scatter.2.cloned.1.call-start = ((), (), s32[]{:S(2)}) async-start(), calls=%async_computation.3 | async-start | bytes 4128768 | tf_op jit(solution)/shard_map/reduce_scatter | solution.py:81
  285.1 1.1 copy-start.2
Sparse Core Ops, SparseCore 0:
  10.1 119.8 all-gather.1
  289.4 54.1 reduce-scatter.1
